TPU v7x, 32 devices: a whole 2x2x4 slice. The times are simulated.
32 devices in a mesh: cfg: 4 (over y, core), dom: 8 (over z, x).
Axes of the slice: x: 2, y: 2, z: 4, core: 2. Of those that a mesh axis runs over, the one named last changes fastest.
Arguments:
- features: bfloat16 [4, 12288, 512], P('cfg', 'dom'), may hold values from -6 to 6
- cotangent: bfloat16 [4, 12288, 512], P('cfg', 'dom'), may hold values from -6 to 6
- w_self: bfloat16 [512, 512], P('cfg'), may hold values from -0.25 to 0.25
- w_neigh: bfloat16 [512, 512], P('cfg'), may hold values from -0.25 to 0.25
- tiles: bfloat16 [64, 128, 128], P('dom'), may hold values from -0.3125 to 0.3125
- edge_peer: int32 [256, 1], P('dom'), may hold values from 0 to 7; in each aligned block of 32 rows (0 to 31, 32 to 63, ...) at most 8 rows name the same one
- edge_src: int32 [256], P('dom'), may hold values from 0 to 11
- edge_dst: int32 [256], P('dom'), may hold values from 0 to 11
- edge_tile: int32 [256], P('dom'), may hold values from 0 to 7
Outputs:
- hidden: bfloat16 [4, 12288, 512], P('cfg', 'dom')
- grad_self: float32 [512, 512], P('cfg')
- grad_neigh: float32 [512, 512], P('cfg')
Inputs may be any that keep to these rules, and one draw needn't show every extreme that they name: `edge_peer`: among the 32 edge blocks of one partition at most 8 have their destination on any one partition, and some destination partition takes exactly 8 of them.
All inputs are finite; a program needn't handle non-finite values.
Results may differ from a plain program's by a relative error of at most 0.0061.
Values may be sent and summed in bfloat16 or wider, within the bound.
No kernel may reach another device: no remote copies, remote signals or barrier semaphores. Data moves between devices by JAX's collectives and lax.ppermute only.
A program may use at most 128 MiB of HBM per device.

v0:
```python
import jax
import jax.numpy as jnp
from jax import lax
from jax.sharding import PartitionSpec as P


def head(pre):
    normed = pre * lax.rsqrt(jnp.mean(pre * pre, -1, keepdims=True) + 1e-05)
    return normed * jax.nn.sigmoid(normed)


def local(features, cotangent, w_self, w_neigh, tiles, edge_peer, edge_src, edge_dst, edge_tile):
    feats = features[0]
    rows, width = feats.shape
    tile = tiles.shape[1]
    blocks = rows // tile
    peers = lax.axis_size("dom")
    edges = edge_src.shape[0]
    per_peer = max(2, 2 * edges // peers)
    slots = peers * per_peer
    target = edge_peer[:, 0]
    peer_hot = (target[:, None] == jnp.arange(peers, dtype=jnp.int32)[None, :]).astype(jnp.int32)
    rank = jnp.sum((jnp.cumsum(peer_hot, 0) - 1) * peer_hot, 1)
    slot = target * per_peer + rank
    slot_hit = slot[:, None] == jnp.arange(slots, dtype=jnp.int32)[None, :]
    place = slot_hit.astype(jnp.bfloat16)
    labels = jnp.sum(jnp.where(slot_hit, (edge_dst + 1)[:, None], 0), 0)
    blocks_x = feats.reshape(blocks, tile, width)
    chosen = blocks_x[edge_src]
    chosen_tiles = tiles[edge_tile]
    partial_value = jnp.einsum(
        "etk,ekd->etd", chosen_tiles, chosen, preferred_element_type=jnp.float32
    ).astype(jnp.bfloat16)
    outgoing = jnp.einsum(
        "es,etd->std", place, partial_value, preferred_element_type=jnp.float32
    ).astype(jnp.bfloat16)
    got, got_labels = (
        lax.all_to_all(
            outgoing.reshape(peers, per_peer, tile, width),
            "dom",
            split_axis=0,
            concat_axis=0,
            tiled=True,
        ),
        lax.all_to_all(
            labels.reshape(peers, per_peer), "dom", split_axis=0, concat_axis=0, tiled=True
        ),
    )
    arrived = got.reshape(slots, tile, width)
    owner_hot = (
        got_labels.reshape(slots)[:, None] - 1 == jnp.arange(blocks, dtype=jnp.int32)[None, :]
    ).astype(jnp.bfloat16)
    aggregate = (
        jnp.einsum("sb,std->btd", owner_hot, arrived, preferred_element_type=jnp.float32)
        .reshape(rows, width)
        .astype(jnp.bfloat16)
    )
    total = jnp.dot(
        feats, lax.all_gather(w_self, "cfg", axis=0, tiled=True), preferred_element_type=jnp.float32
    )
    pre = total + jnp.dot(
        aggregate,
        lax.all_gather(w_neigh, "cfg", axis=0, tiled=True),
        preferred_element_type=jnp.float32,
    )
    out, pullback = jax.vjp(head, pre)
    grad_pre = pullback(cotangent[0].astype(jnp.float32))[0].astype(jnp.bfloat16)
    term_s = lax.dot_general(
        feats, grad_pre, (((0,), (0,)), ((), ())), preferred_element_type=jnp.float32
    )
    term_n = lax.dot_general(
        aggregate, grad_pre, (((0,), (0,)), ((), ())), preferred_element_type=jnp.float32
    )
    total_s, total_n = lax.psum((term_s, term_n), "dom")
    share_s, share_n = (
        lax.psum_scatter(total_s, "cfg", scatter_dimension=0, tiled=True),
        lax.psum_scatter(total_n, "cfg", scatter_dimension=0, tiled=True),
    )
    factor = float(lax.axis_size("cfg") * peers * rows) ** (-0.5)
    return (out.astype(jnp.bfloat16)[None], share_s * factor, share_n * factor)


def solution(mesh):
    placed = (
        P("cfg", "dom", None),
        P("cfg", "dom", None),
        P("cfg", None),
        P("cfg", None),
        P("dom", None, None),
        P("dom", None),
        P("dom"),
        P("dom"),
        P("dom"),
    )
    return jax.shard_map(
        local,
        mesh=mesh,
        in_specs=placed,
        out_specs=(P("cfg", "dom", None), P("cfg", None), P("cfg", None)),
        check_vma=False,
    )
```

profile of v0, /device:TPU:0, one launch (start us, length us, event | category | flops | bytes accessed | tf_op | source)
XLA Modules:
  0.0 381.3 jit_solution(4688032224034469824)
XLA Ops:
  7.2 0.0 copy-start
  7.2 0.8 fusion.19
  8.0 0.1 reduce_window_sum.11
  8.1 0.8 select_reduce_fusion.1
  8.9 0.7 fusion.26
  9.6 0.7 broadcast_add_fusion
  10.2 0.1 select_reduce_fusion
  10.3 0.7 all_to_all.9
  11.0 7.3 %all-to-all-start = ((s32[8,1,8]{2,1,0:T(1,128)}), s32[8,1,8]{2,1,0:T(1,128)S(1)}, u32[]{:S(2)}, u32[]{:S(2)}) async-start(s32[8,1,8]{2,1,0:T(1,128)} %bitcast.4), calls=%async_computation | async-start | bytes 8192 | tf_op jit(solution)/shard_map/all_to_all | solution.py:45
  18.3 0.7 compare_select_fusion
  19.0 0.7 compare_select_fusion.1
  19.6 0.0 copy-done
  19.6 0.0 copy-start.3
  19.6 2.7 gather_fusion.1
  22.4 0.0 copy-done.3
  22.4 0.7 gather_fusion
  23.1 3.4 convolution_convert_fusion
  26.6 6.5 %convert_bitcast_fusion = bf16[8,8,128,512]{3,1,0,2:T(8,128)(2,1)} fusion(bf16[32,128,512]{2,1,0:T(8,128)(2,1)S(1)} %convolution_convert_fusion, s32[32]{0:T(128)S(1)} %fusion.26), kind=kOutput, calls=%fused_computation.5 | convolution fusion | flops 272631808 | bytes 12583040 | tf_op jit(solution)/shard_map/es,etd->std/dot_general | solution.py:34
  33.1 7.4 %copy.25 = bf16[8,8,128,512]{3,1,2,0:T(8,128)(2,1)} copy(bf16[8,8,128,512]{3,1,0,2:T(8,128)(2,1)} %convert_bitcast_fusion) | data formatting | bytes 16777216 | tf_op jit(solution)/shard_map/reshape | solution.py:39
  40.5 0.0 all-to-all-done
  40.5 6.0 %all-to-all-start.1 = ((bf16[8,8,128,512]{3,1,2,0:T(8,128)(2,1)}), bf16[8,8,128,512]{3,1,2,0:T(8,128)(2,1)}, u32[]{:S(2)}, u32[]{:S(2)}) async-start(bf16[8,8,128,512]{3,1,2,0:T(8,128)(2,1)} %copy.25), calls=%async_computation.1 | async-start | bytes 16777216 | tf_op jit(solution)/shard_map/all_to_all | solution.py:38
  46.5 0.0 copy-start.6
  46.5 0.0 copy-start.7
  46.5 0.0 reduce-scatter.5.cloned.1.call-start
  46.6 1.8 copy.28
  48.4 0.0 copy-done.6
  48.4 7.2 %all_gather.6 = bf16[512,512]{1,0:T(8,128)(2,1)S(1)} all-gather(bf16[128,512]{1,0:T(8,128)(2,1)S(1)} %copy-done.6), channel_id=1, replica_groups=mesh['cfg'=4,'dom'=8] {'cfg'}, dimensions={0}, use_global_device_ids=true | all-gather | bytes 655360 | tf_op jit(solution)/shard_map/all_gather | solution.py:59
  55.6 0.0 copy-done.7
  55.6 7.9 %all_gather.7 = bf16[512,512]{1,0:T(8,128)(2,1)} all-gather(bf16[128,512]{1,0:T(8,128)(2,1)S(1)} %copy-done.7), channel_id=1, replica_groups=mesh['cfg'=4,'dom'=8] {'cfg'}, dimensions={0}, use_global_device_ids=true | all-gather | bytes 655360 | tf_op jit(solution)/shard_map/all_gather | solution.py:63
  63.5 2.7 fusion.12
  66.2 0.1 sub.15
  66.3 162.9 %all-to-all-done.1 = bf16[8,8,128,512]{3,1,2,0:T(8,128)(2,1)} async-done(((bf16[8,8,128,512]{3,1,2,0:T(8,128)(2,1)}), bf16[8,8,128,512]{3,1,2,0:T(8,128)(2,1)}, u32[]{:S(2)}, u32[]{:S(2)}) %all-to-all-start.1) | async-done | bytes 8388640 | tf_op jit(solution)/shard_map/all_to_all | solution.py:38
  229.1 4.6 %fusion.7 = bf16[12,128,512]{2,0,1:T(8,128)(2,1)S(1)} fusion(bf16[8,8,128,512]{3,1,2,0:T(8,128)(2,1)} %all-to-all-done.1, s32[64]{0:T(128)S(1)} %sub.15), kind=kOutput, calls=%fused_computation.20 | convolution fusion | flops 101450496 | bytes 9961728 | tf_op jit(solution)/shard_map/sb,std->btd/dot_general | solution.py:54
  233.7 0.0 copy-start.1
  233.7 0.0 copy-start.4
  233.7 0.9 copy.27
  234.6 1.0 copy-done.1
  235.6 0.1 copy-done.4
  235.7 1.1 multiply_reduce_fusion.1
  236.8 1.5 multiply_reduce_fusion
  238.3 2.9 fusion.6
  241.2 0.0 copy-start.5
  241.2 1.2 copy-done.5
  242.3 1.9 fusion.27
  244.3 0.0 reduce-scatter.5.cloned.1.call-update
  244.3 0.0 copy-start.2
  244.3 0.0 reduce-scatter.3.cloned.1.call-start
  244.4 3.5 fusion.15
  247.9 0.0 reduce-scatter.3.cloned.1.call-update
  247.9 0.0 all-reduce.3.cloned.1.call-start
  247.9 20.4 %reduce-scatter.5.cloned.1.call-done = f32[128,512]{0,1:T(8,128)} async-done(((f32[512,512]{0,1:T(8,128)}), f32[128,512]{0,1:T(8,128)}) %reduce-scatter.5.cloned.1.call-update) | async-done | bytes 262160 | tf_op jit(solution)/shard_map/reduce_scatter | solution.py:77
  268.4 27.3 %reduce-scatter.3.cloned.1.call-done = f32[128,512]{0,1:T(8,128)} async-done(((f32[512,512]{0,1:T(8,128)}), f32[128,512]{0,1:T(8,128)}) %reduce-scatter.3.cloned.1.call-update) | async-done | bytes 262160 | tf_op jit(solution)/shard_map/reduce_scatter | solution.py:76
  295.7 0.0 all-reduce.3.cloned.1.call-update
  295.7 0.0 copy-done.2
  295.7 1.6 copy.30
  297.3 74.7 %all-reduce.3.cloned.1.call-done = (f32[128,512]{0,1:T(8,128)}, f32[128,512]{0,1:T(8,128)}) async-done(((f32[128,512]{0,1:T(8,128)}, f32[128,512]{0,1:T(8,128)}), (f32[128,512]{0,1:T(8,128)}, f32[128,512]{0,1:T(8,128)})) %all-reduce.3.cloned.1.call-update) | async-done | bytes 524304 | tf_op jit(solution)/shard_map/psum | solution.py:74
  372.0 1.1 broadcast_multiply_fusion
  373.1 0.8 copy.31
  373.9 0.8 copy.32
  (5 shorter events, 0.1 us)
Async XLA Ops:
  7.2 12.5 %copy-start = (bf16[1,1536,512]{2,1,0:T(8,128)(2,1)S(1)}, bf16[1,1536,512]{2,1,0:T(8,128)(2,1)}, u32[]{:S(2)}) copy-start(bf16[1,1536,512]{2,1,0:T(8,128)(2,1)} %param.9) | copy-start | bytes 4718596
  11.0 29.5 %all-to-all-start = ((s32[8,1,8]{2,1,0:T(1,128)}), s32[8,1,8]{2,1,0:T(1,128)S(1)}, u32[]{:S(2)}, u32[]{:S(2)}) async-start(s32[8,1,8]{2,1,0:T(1,128)} %bitcast.4), calls=%async_computation | async-start | bytes 8192 | tf_op jit(solution)/shard_map/all_to_all | solution.py:45
  19.6 2.8 copy-start.3
  40.5 188.6 %all-to-all-start.1 = ((bf16[8,8,128,512]{3,1,2,0:T(8,128)(2,1)}), bf16[8,8,128,512]{3,1,2,0:T(8,128)(2,1)}, u32[]{:S(2)}, u32[]{:S(2)}) async-start(bf16[8,8,128,512]{3,1,2,0:T(8,128)(2,1)} %copy.25), calls=%async_computation.1 | async-start | bytes 16777216 | tf_op jit(solution)/shard_map/all_to_all | solution.py:38
  46.5 1.8 copy-start.6
  46.5 9.0 %copy-start.7 = (bf16[128,512]{1,0:T(8,128)(2,1)S(1)}, bf16[128,512]{1,0:T(8,128)(2,1)}, u32[]{:S(2)}) copy-start(bf16[128,512]{1,0:T(8,128)(2,1)} %param.12) | copy-start | bytes 393220
  46.5 221.8 %reduce-scatter.5.cloned.1.call-start = ((), (), s32[]{:S(2)}) async-start(), calls=%async_computation.5 | async-start | bytes 1310720 | tf_op jit(solution)/shard_map/reduce_scatter | solution.py:77
  233.7 1.9 copy-start.1
  233.7 2.0 copy-start.4
  241.2 1.2 copy-start.5
  244.3 51.4 %copy-start.2 = (bf16[1,1536,512]{1,2,0:T(8,128)(2,1)S(1)}, bf16[1,1536,512]{1,2,0:T(8,128)(2,1)}, u32[]{:S(2)}) copy-start(bf16[1,1536,512]{1,2,0:T(8,128)(2,1)} %get-tuple-element.15) | copy-start | bytes 4718596
  244.3 51.4 %reduce-scatter.3.cloned.1.call-start = ((), (), s32[]{:S(2)}) async-start(), calls=%async_computation.4 | async-start | bytes 1310720 | tf_op jit(solution)/shard_map/reduce_scatter | solution.py:76
  247.9 124.1 %all-reduce.3.cloned.1.call-start = ((), (), s32[]{:S(2)}) async-start(), calls=%async_computation.6 | async-start | bytes 1048576 | tf_op jit(solution)/shard_map/psum | solution.py:74
Sparse Core Ops, SparseCore 0:
  244.4 23.8 reduce-scatter.4
  270.9 24.7 reduce-scatter.2
  299.2 72.7 all-reduce.2
where the time goes:
time: 382 us; the launch traced here: 381 us
  waiting for transfers between devices  285 us (75%)
  matrix products  23.8 us (6%)
  local copies, waits for them, and re-layouts  19.8 us (5%)
  blocking collectives  15.1 us (4%)
  between operations  13.9 us (4%)
  starting transfers between devices  13.4 us (4%)
  other arithmetic  9.93 us (3%)
    all_to_all x1, waiting for transfers between devices, local(): lax.all_to_all(outgoing.reshape(peers, per_peer, tile, width), 'dom', spl...  163 us
    psum x1, waiting for transfers between devices, local(): total_s, total_n = lax.psum((term_s, term_n), 'dom')  74.7 us
    reduce_scatter x1, waiting for transfers between devices, local(): lax.psum_scatter(total_s, 'cfg', scatter_dimension=0, tiled=True)  27.3 us
    reduce_scatter x1, waiting for transfers between devices, local(): lax.psum_scatter(total_n, 'cfg', scatter_dimension=0, tiled=True)  20.4 us
    all_gather x1, blocking collectives, local(): lax.all_gather(w_neigh, 'cfg', axis=0, tiled=True)  7.89 us
  transfers between devices with their start and end apart: 5, of which 4 were waited for; matrix products, arithmetic and copies ran while one was open for 8% of the time, Pallas kernels for 0%

commit v1 on v0

--- a/solution.py
+++ b/solution.py
@@ -2,6 +2,22 @@
 import jax.numpy as jnp
 from jax import lax
 from jax.sharding import PartitionSpec as P
+
+
+def swapped_with_each(x, axis, split, join):
+    ways, here = (lax.axis_size(axis), lax.axis_index(axis))
+    width = x.shape[split] // ways
+    shape = list(x.shape)
+    shape[split] = width
+    height = shape[join]
+    shape[join] = height * ways
+    full = jnp.zeros(shape, x.dtype)
+    for mask in range(ways):
+        part = lax.dynamic_slice_in_dim(x, (here ^ mask) * width, width, axis=split)
+        if mask:
+            part = lax.ppermute(part, axis, [(d, d ^ mask) for d in range(ways)])
+        full = lax.dynamic_update_slice_in_dim(full, part, (here ^ mask) * height, axis=join)
+    return full
 
 
 def head(pre):
@@ -35,13 +51,7 @@
         "es,etd->std", place, partial_value, preferred_element_type=jnp.float32
     ).astype(jnp.bfloat16)
     got, got_labels = (
-        lax.all_to_all(
-            outgoing.reshape(peers, per_peer, tile, width),
-            "dom",
-            split_axis=0,
-            concat_axis=0,
-            tiled=True,
-        ),
+        swapped_with_each(outgoing.reshape(peers, per_peer, tile, width), "dom", 0, 0),
         lax.all_to_all(
             labels.reshape(peers, per_peer), "dom", split_axis=0, concat_axis=0, tiled=True
         ),

time: 382 us -> 373 us (0.976)
  waiting for transfers between devices: 285 us -> 258 us
  local copies, waits for them, and re-layouts: 19.8 us -> 36.1 us
  starting transfers between devices: 13.4 us -> 18.6 us
    all_to_all x1 -> x0, waiting for transfers between devices: 163 us -> none  [local(): lax.all_to_all(outgoing.reshape(peers, per_peer, tile, width), 'dom', spl...]
    all_to_all x1, waiting for transfers between devices: 0.01 us -> 62.1 us  [local(): lax.all_to_all(labels.reshape(peers, per_peer), 'dom', split_axis=0, conc...]
    ppermute x0 -> x7, waiting for transfers between devices: none -> 44.7 us  [swapped_with_each(): part = lax.ppermute(part, axis, [(d, d ^ mask) for d in range(ways)])]
    reduce_scatter x1, waiting for transfers between devices: 20.4 us -> 49.6 us  [local(): lax.psum_scatter(total_n, 'cfg', scatter_dimension=0, tiled=True)]
    dynamic_update_slice x0 -> x7, local copies, waits for them, and re-layouts: none -> 16.4 us  [swapped_with_each(): lax.dynamic_update_slice_in_dim(full, part, (here ^ mask) * height, axis=...]
    ppermute x0 -> x7, starting transfers between devices: none -> 13.6 us  [swapped_with_each(): part = lax.ppermute(part, axis, [(d, d ^ mask) for d in range(ways)])]
    reshape x1 -> x0, local copies, waits for them, and re-layouts: 7.41 us -> none  [local(): outgoing.reshape(peers, per_peer, tile, width)]
    all_to_all x1 -> x0, starting transfers between devices: 6 us -> none  [local(): lax.all_to_all(outgoing.reshape(peers, per_peer, tile, width), 'dom', spl...]
  transfers between devices with their start and end apart: 5 -> 11, of which waited for: 4 -> 6; matrix products, arithmetic and copies ran while one was open for 8% -> 6% of each run, Pallas kernels for 0% -> 0%
where the time goes in v1:
time: 373 us; the launch traced here: 372 us
  waiting for transfers between devices  258 us (69%)
  local copies, waits for them, and re-layouts  36.1 us (10%)
  matrix products  20.6 us (6%)
  starting transfers between devices  18.6 us (5%)
  blocking collectives  15 us (4%)
  between operations  14 us (4%)
  other arithmetic  9.5 us (3%)
    psum x1, waiting for transfers between devices, local(): total_s, total_n = lax.psum((term_s, term_n), 'dom')  74.7 us
    all_to_all x1, waiting for transfers between devices, local(): lax.all_to_all(labels.reshape(peers, per_peer), 'dom', split_axis=0, conc...  62.1 us
    reduce_scatter x1, waiting for transfers between devices, local(): lax.psum_scatter(total_n, 'cfg', scatter_dimension=0, tiled=True)  49.6 us
    ppermute x7, waiting for transfers between devices, swapped_with_each(): part = lax.ppermute(part, axis, [(d, d ^ mask) for d in range(ways)])  44.7 us
    reduce_scatter x1, waiting for transfers between devices, local(): lax.psum_scatter(total_s, 'cfg', scatter_dimension=0, tiled=True)  27.3 us
    dynamic_update_slice x7, local copies, waits for them, and re-layouts, swapped_with_each(): lax.dynamic_update_slice_in_dim(full, part, (here ^ mask) * height, axis=...  16.4 us
    ppermute x7, starting transfers between devices, swapped_with_each(): part = lax.ppermute(part, axis, [(d, d ^ mask) for d in range(ways)])  13.6 us
    unnamed x24, local copies, waits for them, and re-layouts  10.5 us
  transfers between devices with their start and end apart: 11, of which 6 were waited for; matrix products, arithmetic and copies ran while one was open for 6% of the time, Pallas kernels for 0%

profile of v1, /device:TPU:0, one launch (start us, length us, event | category | flops | bytes accessed | tf_op | source)
XLA Modules:
  0.0 372.3 jit_solution(13885733200684707960)
XLA Ops:
  7.2 0.0 copy-start
  7.2 0.8 fusion.18
  8.0 0.1 reduce_window_sum.11
  8.1 0.8 select_reduce_fusion.1
  8.9 0.7 fusion.25
  9.6 0.7 compare_select_fusion
  10.3 0.0 copy-start.4
  10.4 2.8 gather_fusion.1
  13.1 0.7 gather_fusion
  13.9 3.4 convolution_convert_fusion
  17.3 3.3 convert_bitcast_fusion
  20.6 1.0 broadcast_in_dim.35
  21.7 0.0 copy-start.9
  21.7 0.0 copy-start.7
  21.7 3.0 constant_dynamic-slice_fusion.6
  24.7 3.2 copy-done.1
  27.9 3.0 collective-permute-start
  30.9 1.6 collective-permute-start.1
  32.5 3.0 collective-permute-start.3
  35.5 1.3 collective-permute-start.4
  36.8 0.1 select_reduce_fusion
  36.8 0.7 all_to_all.6
  37.5 4.9 %all-to-all-start = ((s32[8,1,8]{2,1,0:T(1,128)}), s32[8,1,8]{2,1,0:T(1,128)S(1)}, u32[]{:S(2)}, u32[]{:S(2)}) async-start(s32[8,1,8]{2,1,0:T(1,128)} %bitcast.4), calls=%async_computation | async-start | bytes 8192 | tf_op jit(solution)/shard_map/all_to_all | solution.py:55
  42.4 0.0 reduce-scatter.5.cloned.1.call-start
  42.5 7.2 %all_gather.6 = bf16[512,512]{1,0:T(8,128)(2,1)S(1)} all-gather(bf16[128,512]{1,0:T(8,128)(2,1)S(1)} %copy-done.7), channel_id=1, replica_groups=mesh['cfg'=4,'dom'=8] {'cfg'}, dimensions={0}, use_global_device_ids=true | all-gather | bytes 655360 | tf_op jit(solution)/shard_map/all_gather | solution.py:69
  49.7 4.7 %collective-permute-done = bf16[1,8,128,512]{3,1,0,2:T(8,128)(2,1)} collective-permute-done((bf16[1,8,128,512]{3,1,0,2:T(8,128)(2,1)}, bf16[1,8,128,512]{3,1,0,2:T(8,128)(2,1)}, u32[]{:S(2)}, u32[]{:S(2)}) %collective-permute-start) | collective-permute-done | bytes 1048608 | tf_op jit(solution)/shard_map/ppermute | solution.py:18
  54.4 3.9 %collective-permute-start.5 = (bf16[1,8,128,512]{3,1,0,2:T(8,128)(2,1)}, bf16[1,8,128,512]{3,1,0,2:T(8,128)(2,1)}, u32[]{:S(2)}, u32[]{:S(2)}) collective-permute-start(bf16[1,8,128,512]{3,1,0,2:T(8,128)(2,1)} %get-tuple-element.15), channel_id=1, source_target_pairs={{0,6},{1,7},{2,4},{3,5},{4,2},{5,3},{6,0},{7,1},{8,14},{9,15},{10,... | collective-permute-start | bytes 3145736 | tf_op jit(solution)/shard_map/ppermute | solution.py:18
  58.2 2.8 fusion.11
  61.0 40.0 %collective-permute-done.1 = bf16[1,8,128,512]{3,1,0,2:T(8,128)(2,1)} collective-permute-done((bf16[1,8,128,512]{3,1,0,2:T(8,128)(2,1)S(1)}, bf16[1,8,128,512]{3,1,0,2:T(8,128)(2,1)}, u32[]{:S(2)}, u32[]{:S(2)}) %collective-permute-start.1) | collective-permute-done | bytes 1048608 | tf_op jit(solution)/shard_map/ppermute | solution.py:18
  101.0 0.9 collective-permute-start.6
  101.9 7.8 %all_gather.7 = bf16[512,512]{1,0:T(8,128)(2,1)} all-gather(bf16[128,512]{1,0:T(8,128)(2,1)S(1)} %copy-done.8), channel_id=1, replica_groups=mesh['cfg'=4,'dom'=8] {'cfg'}, dimensions={0}, use_global_device_ids=true | all-gather | bytes 655360 | tf_op jit(solution)/shard_map/all_gather | solution.py:73
  109.7 1.7 copy.26
  111.4 62.1 %all-to-all-done = s32[8,1,8]{2,1,0:T(1,128)S(1)} async-done(((s32[8,1,8]{2,1,0:T(1,128)}), s32[8,1,8]{2,1,0:T(1,128)S(1)}, u32[]{:S(2)}, u32[]{:S(2)}) %all-to-all-start) | async-done | bytes 288 | tf_op jit(solution)/shard_map/all_to_all | solution.py:55
  173.5 0.1 sub.15
  173.6 2.4 constant_dynamic-update-slice_fusion.5
  175.9 2.3 constant_dynamic-update-slice_fusion.4
  178.3 2.4 constant_dynamic-update-slice_fusion.3
  180.6 2.4 constant_dynamic-update-slice_fusion.2
  183.0 2.3 constant_dynamic-update-slice_fusion.1
  185.3 2.4 constant_dynamic-update-slice_fusion
  187.7 2.3 constant_dynamic-update-slice_fusion.6
  190.0 4.6 %fusion.6 = bf16[12,128,512]{2,0,1:T(8,128)(2,1)S(1)} fusion(bf16[8,8,128,512]{3,1,0,2:T(8,128)(2,1)} %constant_dynamic-update-slice_fusion.6, s32[64]{0:T(128)S(1)} %sub.15), kind=kOutput, calls=%fused_computation.19 | convolution fusion | flops 101450496 | bytes 9961728 | tf_op jit(solution)/shard_map/sb,std->btd/dot_general | solution.py:64
  194.7 0.9 copy.25
  195.5 1.0 copy-done.2
  196.5 0.1 copy-done.5
  196.6 1.1 multiply_reduce_fusion.1
  197.7 1.5 multiply_reduce_fusion
  199.3 2.9 fusion.5
  202.1 1.1 copy-done.6
  203.3 2.0 fusion.26
  205.2 0.0 reduce-scatter.5.cloned.1.call-update
  205.2 0.0 reduce-scatter.3.cloned.1.call-start
  205.3 3.5 fusion.14
  208.8 0.0 reduce-scatter.3.cloned.1.call-update
  208.8 0.0 all-reduce.3.cloned.1.call-start
  208.8 49.6 %reduce-scatter.5.cloned.1.call-done = f32[128,512]{0,1:T(8,128)} async-done(((f32[512,512]{0,1:T(8,128)}), f32[128,512]{0,1:T(8,128)}) %reduce-scatter.5.cloned.1.call-update) | async-done | bytes 262160 | tf_op jit(solution)/shard_map/reduce_scatter | solution.py:87
  258.5 27.3 %reduce-scatter.3.cloned.1.call-done = f32[128,512]{0,1:T(8,128)} async-done(((f32[512,512]{0,1:T(8,128)}), f32[128,512]{0,1:T(8,128)}) %reduce-scatter.3.cloned.1.call-update) | async-done | bytes 262160 | tf_op jit(solution)/shard_map/reduce_scatter | solution.py:86
  285.8 0.0 all-reduce.3.cloned.1.call-update
  285.8 1.6 copy.28
  287.4 74.7 %all-reduce.3.cloned.1.call-done = (f32[128,512]{0,1:T(8,128)}, f32[128,512]{0,1:T(8,128)}) async-done(((f32[128,512]{0,1:T(8,128)}, f32[128,512]{0,1:T(8,128)}), (f32[128,512]{0,1:T(8,128)}, f32[128,512]{0,1:T(8,128)})) %all-reduce.3.cloned.1.call-update) | async-done | bytes 524304 | tf_op jit(solution)/shard_map/psum | solution.py:84
  362.2 1.0 broadcast_multiply_fusion.1
  363.1 0.8 copy.29
  364.0 1.0 broadcast_multiply_fusion
  365.0 0.8 copy.30
  (24 shorter events, 0.1 us)
Async XLA Ops:
  7.2 3.2 copy-start
  10.3 2.8 copy-start.4
  21.7 15.1 %copy-start.9 = (s32[32]{0:T(128)S(1)}, s32[32]{0:T(128)}, u32[]{:S(2)}) copy-start(s32[32]{0:T(128)} %param.16) | copy-start | bytes 388
  21.7 20.8 %copy-start.7 = (bf16[128,512]{1,0:T(8,128)(2,1)S(1)}, bf16[128,512]{1,0:T(8,128)(2,1)}, u32[]{:S(2)}) copy-start(bf16[128,512]{1,0:T(8,128)(2,1)} %param.11) | copy-start | bytes 393220
  24.7 3.2 copy-start.1
  27.9 26.4 %collective-permute-start = (bf16[1,8,128,512]{3,1,0,2:T(8,128)(2,1)}, bf16[1,8,128,512]{3,1,0,2:T(8,128)(2,1)}, u32[]{:S(2)}, u32[]{:S(2)}) collective-permute-start(bf16[1,8,128,512]{3,1,0,2:T(8,128)(2,1)} %get-tuple-element.20), channel_id=1, source_target_pairs={{0,1},{1,0},{2,3},{3,2},{4,5},{5,4},{6,7},{7,6},{8,9},{9,8},{10,11... | collective-permute-start | bytes 3145736 | tf_op jit(solution)/shard_map/ppermute | solution.py:18
  30.9 70.1 %collective-permute-start.1 = (bf16[1,8,128,512]{3,1,0,2:T(8,128)(2,1)S(1)}, bf16[1,8,128,512]{3,1,0,2:T(8,128)(2,1)}, u32[]{:S(2)}, u32[]{:S(2)}) collective-permute-start(bf16[1,8,128,512]{3,1,0,2:T(8,128)(2,1)S(1)} %get-tuple-element.19), channel_id=1, source_target_pairs={{0,2},{1,3},{2,0},{3,1},{4,6},{5,7},{6,4},{7,5},{8,10},{9,11},{10,... | collective-permute-start | bytes 3145736 | tf_op jit(solution)/shard_map/ppermute | solution.py:18
  32.5 145.8 %collective-permute-start.2 = (bf16[1,8,128,512]{3,1,0,2:T(8,128)(2,1)}, bf16[1,8,128,512]{3,1,0,2:T(8,128)(2,1)}, u32[]{:S(2)}, u32[]{:S(2)}) collective-permute-start(bf16[1,8,128,512]{3,1,0,2:T(8,128)(2,1)} %get-tuple-element.18), channel_id=1, source_target_pairs={{0,3},{1,2},{2,1},{3,0},{4,7},{5,6},{6,5},{7,4},{8,11},{9,10},{10,... | collective-permute-start | bytes 3145736 | tf_op jit(solution)/shard_map/ppermute | solution.py:18
  32.5 148.2 %collective-permute-start.3 = (bf16[1,8,128,512]{3,1,0,2:T(8,128)(2,1)}, bf16[1,8,128,512]{3,1,0,2:T(8,128)(2,1)}, u32[]{:S(2)}, u32[]{:S(2)}) collective-permute-start(bf16[1,8,128,512]{3,1,0,2:T(8,128)(2,1)} %get-tuple-element.17), channel_id=1, source_target_pairs={{0,4},{1,5},{2,6},{3,7},{4,0},{5,1},{6,2},{7,3},{8,12},{9,13},{10,... | collective-permute-start | bytes 3145736 | tf_op jit(solution)/shard_map/ppermute | solution.py:18
  35.5 147.5 %collective-permute-start.4 = (bf16[1,8,128,512]{3,1,0,2:T(8,128)(2,1)}, bf16[1,8,128,512]{3,1,0,2:T(8,128)(2,1)}, u32[]{:S(2)}, u32[]{:S(2)}) collective-permute-start(bf16[1,8,128,512]{3,1,0,2:T(8,128)(2,1)} %get-tuple-element.16), channel_id=1, source_target_pairs={{0,5},{1,4},{2,7},{3,6},{4,1},{5,0},{6,3},{7,2},{8,13},{9,12},{10,... | collective-permute-start | bytes 3145736 | tf_op jit(solution)/shard_map/ppermute | solution.py:18
  37.5 135.9 %all-to-all-start = ((s32[8,1,8]{2,1,0:T(1,128)}), s32[8,1,8]{2,1,0:T(1,128)S(1)}, u32[]{:S(2)}, u32[]{:S(2)}) async-start(s32[8,1,8]{2,1,0:T(1,128)} %bitcast.4), calls=%async_computation | async-start | bytes 8192 | tf_op jit(solution)/shard_map/all_to_all | solution.py:55
  42.4 216.1 %reduce-scatter.5.cloned.1.call-start = ((), (), s32[]{:S(2)}) async-start(), calls=%async_computation.4 | async-start | bytes 1310720 | tf_op jit(solution)/shard_map/reduce_scatter | solution.py:87
  54.4 47.5 %copy-start.8 = (bf16[128,512]{1,0:T(8,128)(2,1)S(1)}, bf16[128,512]{1,0:T(8,128)(2,1)}, u32[]{:S(2)}) copy-start(bf16[128,512]{1,0:T(8,128)(2,1)} %param.12) | copy-start | bytes 393220
  54.4 130.9 %collective-permute-start.5 = (bf16[1,8,128,512]{3,1,0,2:T(8,128)(2,1)}, bf16[1,8,128,512]{3,1,0,2:T(8,128)(2,1)}, u32[]{:S(2)}, u32[]{:S(2)}) collective-permute-start(bf16[1,8,128,512]{3,1,0,2:T(8,128)(2,1)} %get-tuple-element.15), channel_id=1, source_target_pairs={{0,6},{1,7},{2,4},{3,5},{4,2},{5,3},{6,0},{7,1},{8,14},{9,15},{10,... | collective-permute-start | bytes 3145736 | tf_op jit(solution)/shard_map/ppermute | solution.py:18
  101.0 86.7 %collective-permute-start.6 = (bf16[1,8,128,512]{3,1,0,2:T(8,128)(2,1)}, bf16[1,8,128,512]{3,1,0,2:T(8,128)(2,1)}, u32[]{:S(2)}, u32[]{:S(2)}) collective-permute-start(bf16[1,8,128,512]{3,1,0,2:T(8,128)(2,1)} %get-tuple-element.14), channel_id=1, source_target_pairs={{0,7},{1,6},{2,5},{3,4},{4,3},{5,2},{6,1},{7,0},{8,15},{9,14},{10,... | collective-permute-start | bytes 3145736 | tf_op jit(solution)/shard_map/ppermute | solution.py:18
  194.6 1.9 copy-start.2
  194.6 2.0 copy-start.5
  202.1 1.1 copy-start.6
  205.2 80.6 %copy-start.3 = (bf16[1,1536,512]{1,2,0:T(8,128)(2,1)S(1)}, bf16[1,1536,512]{1,2,0:T(8,128)(2,1)}, u32[]{:S(2)}) copy-start(bf16[1,1536,512]{1,2,0:T(8,128)(2,1)} %get-tuple-element.23) | copy-start | bytes 4718596
  205.2 80.6 %reduce-scatter.3.cloned.1.call-start = ((), (), s32[]{:S(2)}) async-start(), calls=%async_computation.3 | async-start | bytes 1310720 | tf_op jit(solution)/shard_map/reduce_scatter | solution.py:86
  208.8 153.4 %all-reduce.3.cloned.1.call-start = ((), (), s32[]{:S(2)}) async-start(), calls=%async_computation.5 | async-start | bytes 1048576 | tf_op jit(solution)/shard_map/psum | solution.py:84
Sparse Core Ops, SparseCore 0:
  205.4 53.0 reduce-scatter.4
  261.0 24.7 reduce-scatter.2
  289.3 72.8 all-reduce.2
